TPU v7x, 32 devices: a whole 2x2x4 slice. The times are simulated.
32 devices in a mesh: dp: 16 (over z, y, x), tensor: 2 (over core).
Axes of the slice: x: 2, y: 2, z: 4, core: 2. Of those that a mesh axis runs over, the one named last changes fastest.
Arguments:
- tokens: bfloat16 [24576, 768], P(('dp', 'tensor')), may hold values from -6 to 6
- kept_patches: int32 [24576], P(('dp', 'tensor')), may hold values from 0 to 1567, as said below
- clip_lengths: int32 [128], replicated, may hold values from 39 to 314, as said below
- clip_device: int32 [128], replicated, may hold values from 0 to 31, as said below
- cot_output: bfloat16 [24576, 768], P(('dp', 'tensor')), may hold values from -6 to 6
- cot_aligned: bfloat16 [24576, 1024], P(('dp', 'tensor')), may hold values from -6 to 6
- entry_weight: float32 [1769472], P(('dp', 'tensor')), may hold values from -0.21875 to 0.21875
- entry_first: float32 [1769472], P(('dp', 'tensor')), may hold values from -112 to 112
- entry_second: float32 [1769472], P(('dp', 'tensor')), may hold values from 245.76 to 4096.8193
- exit_weight: float32 [589824], P(('dp', 'tensor')), may hold values from -1.75 to 1.75
- exit_first: float32 [589824], P(('dp', 'tensor')), may hold values from -24 to 24
- exit_second: float32 [589824], P(('dp', 'tensor')), may hold values from 12.288 to 204.71808
- align_weight: float32 [786432], P(('dp', 'tensor')), may hold values from -0.21875 to 0.21875
- align_first: float32 [786432], P(('dp', 'tensor')), may hold values from -128 to 128
- align_second: float32 [786432], P(('dp', 'tensor')), may hold values from 447.2832 to 8183.808
- expand_weight: float32 [3072, 768], P(('dp', 'tensor')), may hold values from -0.21875 to 0.21875
- expand_first: float32 [3072, 768], P(('dp', 'tensor')), may hold values from -32 to 32
- expand_second: float32 [3072, 768], P(('dp', 'tensor')), may hold values from 24.576 to 409.68192
- reduce_weight: float32 [3072, 768], P(('dp', 'tensor')), may hold values from -0.109375 to 0.109375
- reduce_first: float32 [3072, 768], P(('dp', 'tensor')), may hold values from -80 to 80
- reduce_second: float32 [3072, 768], P(('dp', 'tensor')), may hold values from 144.50688 to 2457.6
- position_table: float32 [1204224], P(('dp', 'tensor')), may hold values from -3 to 3
- position_first: float32 [1204224], P(('dp', 'tensor')), may hold values from -5 to 5
- position_second: float32 [1204224], P(('dp', 'tensor')), may hold values from 0.5219265 to 7.836735
- norm_params: float32 [3072], P(('dp', 'tensor')), may hold values from -1.5 to 1.5, as said below
- norm_first: float32 [3072], P(('dp', 'tensor')), may hold values from -128 to 128
- norm_second: float32 [3072], P(('dp', 'tensor')), may hold values from 447.2832 to 8183.808
Outputs:
- block_out: bfloat16 [24576, 768], P(('dp', 'tensor'))
- aligned: bfloat16 [24576, 1024], P(('dp', 'tensor'))
- token_grad: float32 [24576, 768], P(('dp', 'tensor'))
- new_entry_first: float32 [1769472], P(('dp', 'tensor'))
- new_entry_second: float32 [1769472], P(('dp', 'tensor'))
- new_entry_weight: float32 [1769472], P(('dp', 'tensor'))
- new_exit_first: float32 [589824], P(('dp', 'tensor'))
- new_exit_second: float32 [589824], P(('dp', 'tensor'))
- new_exit_weight: float32 [589824], P(('dp', 'tensor'))
- new_align_first: float32 [786432], P(('dp', 'tensor'))
- new_align_second: float32 [786432], P(('dp', 'tensor'))
- new_align_weight: float32 [786432], P(('dp', 'tensor'))
- new_expand_first: float32 [3072, 768], P(('dp', 'tensor'))
- new_expand_second: float32 [3072, 768], P(('dp', 'tensor'))
- new_expand_weight: float32 [3072, 768], P(('dp', 'tensor'))
- new_reduce_first: float32 [3072, 768], P(('dp', 'tensor'))
- new_reduce_second: float32 [3072, 768], P(('dp', 'tensor'))
- new_reduce_weight: float32 [3072, 768], P(('dp', 'tensor'))
- new_position_first: float32 [1204224], P(('dp', 'tensor'))
- new_position_second: float32 [1204224], P(('dp', 'tensor'))
- new_position_table: float32 [1204224], P(('dp', 'tensor'))
- new_norm_first: float32 [3072], P(('dp', 'tensor'))
- new_norm_second: float32 [3072], P(('dp', 'tensor'))
- new_norm_params: float32 [3072], P(('dp', 'tensor'))
- lamb_stats: float32 [3, 7], replicated
Inputs may be any that keep to these rules, and one draw needn't show every extreme that they name: `clip_lengths`: every clip has 314 rows (a video clip) or 39 rows (an image). `clip_device`: each device index d = i * 2 + j holds exactly 4 clips, at most 2 of them video clips, and some device holds 2. `kept_patches`: within a video clip the rows hold distinct positions below 1568 in rising order, within an image distinct positions below 196 in rising order; padding rows hold 0. `norm_params`: gains lie in 0.5 to 1.5; shifts are normal of deviation 0.5, held within -1.5 to 1.5.
All inputs are finite; a program needn't handle non-finite values.
Results may differ from a plain program's by a relative error of at most 0.0085.
The roundings to bfloat16 on the way count: a program that leaves them out, or rounds other values in their place, can miss the bound.
Values may be sent and summed in bfloat16 or wider, within the bound.
A program may use at most 192 MiB of HBM per device.

v0:
```python
import jax
import jax.numpy as jnp
from jax import lax
from jax.sharding import PartitionSpec as P

H = 12
HD = 64
LN_EPS = 1e-06
MASKED = -1e30
RATE = 0.5
BETA_ONE = 0.9
BETA_TWO = 0.98
ADAM_EPS = 1e-06
DECAY = 0.05
TINY = 1e-06


def contract(left, right, left_dim, right_dim):
    return lax.dot_general(
        left, right, (((left_dim,), (right_dim,)), ((), ())), preferred_element_type=jnp.float32
    )


def layer_norm(values, gain, shift):
    center = values - jnp.mean(values, axis=-1, keepdims=True)
    spread = jnp.mean(center * center, axis=-1, keepdims=True)
    return center * lax.rsqrt(spread + LN_EPS) * gain + shift


def gelu_exact(values):
    return jax.nn.gelu(values, approximate=False)


def row_layout(clip_lengths, clip_device, device, row_count):
    mine = clip_device == device
    own_length = jnp.where(mine, clip_lengths, 0)
    starts = jnp.cumsum(own_length) - own_length
    filled = jnp.sum(own_length)
    positions = jnp.arange(row_count, dtype=jnp.int32)
    begun = mine[None, :] & (starts[None, :] <= positions[:, None])
    segment = jnp.sum(begun.astype(jnp.int32), axis=1)
    valid_rows = positions < filled
    return (jnp.where(valid_rows, segment, 0), valid_rows)


def head_scores(queries, key_rows, same_clip, score_scale):
    scores = contract(queries, key_rows, 1, 1) * score_scale
    return jnp.where(same_clip, scores, MASKED)


def head_forward(queries, key_rows, value_rows, same_clip, score_scale):
    scores = head_scores(queries, key_rows, same_clip, score_scale)
    peak_score = jnp.max(scores, axis=1, keepdims=True)
    raised = jnp.exp(scores - peak_score)
    row_total = jnp.sum(raised, axis=1, keepdims=True)
    attention = raised / row_total
    result = jnp.dot(attention.astype(jnp.bfloat16), value_rows, preferred_element_type=jnp.float32)
    return (result, (peak_score + jnp.log(row_total))[:, 0])


def head_backward(queries, key_rows, value_rows, log_total, grad_heads, same_clip, score_scale):
    scores = head_scores(queries, key_rows, same_clip, score_scale)
    attention = jnp.exp(scores - log_total[:, None])
    attention_low = attention.astype(jnp.bfloat16)
    grad_values = contract(attention_low, grad_heads, 0, 0)
    grad_attention = contract(grad_heads, value_rows, 1, 1)
    inner = jnp.sum(attention * grad_attention, axis=1, keepdims=True)
    grad_score = (attention * (grad_attention - inner)).astype(jnp.bfloat16)
    grad_queries = jnp.dot(grad_score, key_rows, preferred_element_type=jnp.float32) * score_scale
    grad_keys = contract(grad_score, queries, 0, 0) * score_scale
    return (grad_queries, grad_keys, grad_values)


def lamb_moments(weight, gradient, first, second, decay):
    new_first = BETA_ONE * first + (1.0 - BETA_ONE) * gradient
    new_second = BETA_TWO * second + (1.0 - BETA_TWO) * gradient * gradient
    update = new_first / (jnp.sqrt(new_second) + ADAM_EPS) + decay * weight
    return (new_first, new_second, update)


def local(
    tokens,
    kept_patches,
    clip_lengths,
    clip_device,
    cot_output,
    cot_aligned,
    entry_weight,
    entry_first,
    entry_second,
    exit_weight,
    exit_first,
    exit_second,
    align_weight,
    align_first,
    align_second,
    expand_weight,
    expand_first,
    expand_second,
    reduce_weight,
    reduce_first,
    reduce_second,
    position_table,
    position_first,
    position_second,
    norm_params,
    norm_first,
    norm_second,
):
    row_count, model_width = tokens.shape
    align_width = cot_aligned.shape[1]
    score_scale = HD ** (-0.5)
    masters = (
        entry_weight,
        exit_weight,
        align_weight,
        expand_weight,
        reduce_weight,
        position_table,
        norm_params,
    )
    device = lax.axis_index("dp") * lax.axis_size("tensor") + lax.axis_index("tensor")
    segment, valid_rows = row_layout(clip_lengths, clip_device, device, row_count)
    same_clip = segment[:, None] == segment[None, :]
    valid_column = valid_rows[:, None]
    gathered = (
        lax.all_gather(entry_weight.astype(jnp.bfloat16), ("dp", "tensor"), axis=0, tiled=True),
        lax.all_gather(exit_weight.astype(jnp.bfloat16), ("dp", "tensor"), axis=0, tiled=True),
        lax.all_gather(align_weight.astype(jnp.bfloat16), ("dp", "tensor"), axis=0, tiled=True),
        lax.all_gather(position_table.astype(jnp.bfloat16), ("dp", "tensor"), axis=0, tiled=True),
        lax.all_gather(norm_params.astype(jnp.bfloat16), ("dp", "tensor"), axis=0, tiled=True),
    )
    expand_low, reduce_low = (
        lax.all_gather(expand_weight.astype(jnp.bfloat16), "dp", axis=0, tiled=True),
        lax.all_gather(reduce_weight.astype(jnp.bfloat16), "dp", axis=0, tiled=True),
    )
    entry_low = gathered[0].reshape(model_width, 3 * model_width)
    exit_low = gathered[1].reshape(model_width, model_width)
    align_low = gathered[2].reshape(model_width, align_width)
    table_low = gathered[3].reshape(-1, model_width)
    norm_low = gathered[4].astype(jnp.float32).reshape(4, model_width)
    residual = tokens.astype(jnp.float32) + jnp.take(table_low, kept_patches, axis=0).astype(
        jnp.float32
    )
    normed_one = layer_norm(residual, norm_low[0], norm_low[1]).astype(jnp.bfloat16)
    joint_low = jnp.dot(normed_one, entry_low, preferred_element_type=jnp.float32).astype(
        jnp.bfloat16
    )
    split_heads = joint_low.reshape(row_count, 3, H, HD).transpose(1, 2, 0, 3)
    head_outputs, log_totals = lax.map(
        lambda entries: head_forward(entries[0], entries[1], entries[2], same_clip, score_scale),
        (split_heads[0], split_heads[1], split_heads[2]),
    )
    attended = head_outputs.transpose(1, 0, 2).reshape(row_count, model_width).astype(jnp.bfloat16)
    middle = residual + jnp.dot(attended, exit_low, preferred_element_type=jnp.float32)
    normed_two = layer_norm(middle, norm_low[2], norm_low[3]).astype(jnp.bfloat16)
    hidden_in = lax.all_gather(normed_two, "tensor", axis=0, tiled=True)
    hidden_pre = contract(hidden_in, expand_low, 1, 1)
    hidden_act = gelu_exact(hidden_pre).astype(jnp.bfloat16)
    feed_out = lax.psum_scatter(
        jnp.dot(hidden_act, reduce_low, preferred_element_type=jnp.float32).astype(jnp.bfloat16),
        "tensor",
        scatter_dimension=0,
        tiled=True,
    ).astype(jnp.float32)
    out_low = (middle + feed_out).astype(jnp.bfloat16)
    block_out = jnp.where(valid_column, out_low, jnp.zeros_like(out_low))
    align_rows = jnp.dot(out_low, align_low, preferred_element_type=jnp.float32).astype(
        jnp.bfloat16
    )
    aligned = jnp.where(valid_column, align_rows, jnp.zeros_like(align_rows))
    cot_align_valid = jnp.where(valid_column, cot_aligned, jnp.zeros_like(cot_aligned))
    grad_align = contract(out_low, cot_align_valid, 0, 0)
    grad_out = jnp.where(valid_column, cot_output.astype(jnp.float32), 0.0) + contract(
        cot_align_valid, align_low, 1, 1
    )
    grad_feed = grad_out.astype(jnp.bfloat16)
    grad_feed_rows = lax.all_gather(grad_feed, "tensor", axis=0, tiled=True)
    grad_act = contract(grad_feed_rows, reduce_low, 1, 1)
    gelu_value, gelu_back = jax.vjp(gelu_exact, hidden_pre)
    grad_pre = gelu_back(grad_act)[0].astype(jnp.bfloat16)
    grad_reduce = contract(hidden_act, grad_feed_rows, 0, 0)
    grad_expand = contract(grad_pre, hidden_in, 0, 0)
    grad_two = lax.psum_scatter(
        jnp.dot(grad_pre, expand_low, preferred_element_type=jnp.float32),
        "tensor",
        scatter_dimension=0,
        tiled=True,
    )
    grad_expand, grad_reduce = (
        lax.psum_scatter(grad_expand, "dp", scatter_dimension=0, tiled=True),
        lax.psum_scatter(grad_reduce, "dp", scatter_dimension=0, tiled=True),
    )
    norm_value, norm_back_two = jax.vjp(layer_norm, middle, norm_low[2], norm_low[3])
    grad_from_two, grad_gain_two, grad_shift_two = norm_back_two(grad_two)
    grad_middle = grad_out + grad_from_two
    grad_branch = grad_middle.astype(jnp.bfloat16)
    grad_exit = contract(attended, grad_branch, 0, 0)
    grad_attended = contract(grad_branch, exit_low, 1, 1).astype(jnp.bfloat16)
    grad_heads = grad_attended.reshape(row_count, H, HD).transpose(1, 0, 2)
    grad_queries, grad_keys, grad_values = lax.map(
        lambda entries: head_backward(
            entries[0], entries[1], entries[2], entries[3], entries[4], same_clip, score_scale
        ),
        (split_heads[0], split_heads[1], split_heads[2], log_totals, grad_heads),
    )
    grad_joint = jnp.stack((grad_queries, grad_keys, grad_values)).transpose(2, 0, 1, 3)
    grad_joint = grad_joint.reshape(row_count, 3 * model_width).astype(jnp.bfloat16)
    grad_entry = contract(normed_one, grad_joint, 0, 0)
    grad_one = contract(grad_joint, entry_low, 1, 1)
    norm_value_one, norm_back_one = jax.vjp(layer_norm, residual, norm_low[0], norm_low[1])
    grad_from_one, grad_gain_one, grad_shift_one = norm_back_one(grad_one)
    token_grad = grad_middle + grad_from_one
    grad_table = jax.ops.segment_sum(token_grad, kept_patches, num_segments=table_low.shape[0])
    grad_norms = jnp.concatenate((grad_gain_one, grad_shift_one, grad_gain_two, grad_shift_two))
    summed = (
        lax.psum_scatter(grad_entry.reshape(-1), ("dp", "tensor"), scatter_dimension=0, tiled=True),
        lax.psum_scatter(grad_exit.reshape(-1), ("dp", "tensor"), scatter_dimension=0, tiled=True),
        lax.psum_scatter(grad_align.reshape(-1), ("dp", "tensor"), scatter_dimension=0, tiled=True),
        lax.psum_scatter(grad_table.reshape(-1), ("dp", "tensor"), scatter_dimension=0, tiled=True),
        lax.psum_scatter(grad_norms, ("dp", "tensor"), scatter_dimension=0, tiled=True),
    )
    gradients = (summed[0], summed[1], summed[2], grad_expand, grad_reduce, summed[3], summed[4])
    firsts = (
        entry_first,
        exit_first,
        align_first,
        expand_first,
        reduce_first,
        position_first,
        norm_first,
    )
    seconds = (
        entry_second,
        exit_second,
        align_second,
        expand_second,
        reduce_second,
        position_second,
        norm_second,
    )
    decays = (DECAY, DECAY, DECAY, DECAY, DECAY, DECAY, 0.0)
    results = [
        lamb_moments(
            masters[member], gradients[member], firsts[member], seconds[member], decays[member]
        )
        for member in range(7)
    ]
    update_local = jnp.stack([jnp.sum(found[2] * found[2]) for found in results])
    weight_squares, update_squares = lax.psum(
        (jnp.stack([jnp.sum(master * master) for master in masters]), update_local),
        ("dp", "tensor"),
    )
    trust = jnp.sqrt(weight_squares) / jnp.sqrt(update_squares + TINY)
    outputs = [block_out, aligned, token_grad]
    for member in range(7):
        found = results[member]
        outputs = outputs + [found[0], found[1], masters[member] - RATE * trust[member] * found[2]]
    lamb_stats = jnp.stack((trust, jnp.sqrt(weight_squares), jnp.sqrt(update_squares)))
    outputs = outputs + [lamb_stats]
    return tuple(outputs)


def solution(mesh):
    placed = (
        P(("dp", "tensor"), None),
        P(("dp", "tensor")),
        P(),
        P(),
        P(("dp", "tensor"), None),
        P(("dp", "tensor"), None),
        P(("dp", "tensor")),
        P(("dp", "tensor")),
        P(("dp", "tensor")),
        P(("dp", "tensor")),
        P(("dp", "tensor")),
        P(("dp", "tensor")),
        P(("dp", "tensor")),
        P(("dp", "tensor")),
        P(("dp", "tensor")),
        P(("dp", "tensor"), None),
        P(("dp", "tensor"), None),
        P(("dp", "tensor"), None),
        P(("dp", "tensor"), None),
        P(("dp", "tensor"), None),
        P(("dp", "tensor"), None),
        P(("dp", "tensor")),
        P(("dp", "tensor")),
        P(("dp", "tensor")),
        P(("dp", "tensor")),
        P(("dp", "tensor")),
        P(("dp", "tensor")),
    )
    return jax.shard_map(
        local,
        mesh=mesh,
        in_specs=placed,
        out_specs=(
            P(("dp", "tensor"), None),
            P(("dp", "tensor"), None),
            P(("dp", "tensor"), None),
            P(("dp", "tensor")),
            P(("dp", "tensor")),
            P(("dp", "tensor")),
            P(("dp", "tensor")),
            P(("dp", "tensor")),
            P(("dp", "tensor")),
            P(("dp", "tensor")),
            P(("dp", "tensor")),
            P(("dp", "tensor")),
            P(("dp", "tensor"), None),
            P(("dp", "tensor"), None),
            P(("dp", "tensor"), None),
            P(("dp", "tensor"), None),
            P(("dp", "tensor"), None),
            P(("dp", "tensor"), None),
            P(("dp", "tensor")),
            P(("dp", "tensor")),
            P(("dp", "tensor")),
            P(("dp", "tensor")),
            P(("dp", "tensor")),
            P(("dp", "tensor")),
            P(),
        ),
        check_vma=False,
    )
```

profile of v0, /device:TPU:0, one launch (start us, length us, event | category | flops | bytes accessed | tf_op | source)
XLA Modules:
  0.0 1165.3 jit_solution(5532540820435427545)
XLA Ops:
  19.3 42.3 %all-reduce = bf16[3072]{0:T(1024)(128)(2,1)S(1)} all-reduce(bf16[3072]{0:T(1024)(128)(2,1)S(1)} %dynamic-update-slice), channel_id=1, replica_groups=mesh['dp'=16,'tensor'=2] {'dp','tensor'}, use_global_device_ids=true, to_apply=%add | all-reduce | flops 3072 | bytes 12288
  64.1 4.3 all-gather.12.cloned.1.call-done
  68.4 3.3 reshape.249
  71.7 63.2 %all-gather.24.cloned.1.call-done = bf16[32,1,37632]{2,1,0:T(2,128)(2,1)} async-done(((bf16[1,1,37632]{2,1,0:T(2,128)(2,1)}), bf16[32,1,37632]{2,1,0:T(2,128)(2,1)}) %all-gather.24.cloned.1.call-update) | async-done | bytes 2408464 | tf_op jit(solution)/shard_map/all_gather | solution.py:130
  135.0 51.2 %reduce.1 = bf16[32,37632]{1,0:T(8,128)(2,1)} reduce(bf16[32,1,37632]{2,1,0:T(2,128)(2,1)} %all-gather.24.cloned.1.call-done, bf16[]{:T(256)} %constant.226), dimensions={1}, to_apply=%all-gather.reduce_sub_computation | reduce | bytes 4816898 | tf_op jit(solution)/shard_map/all_gather | solution.py:130
  186.1 5.0 reshape.244
  191.1 3.4 gather_fusion
  197.4 7.6 reshape.245
  205.0 7.2 convolution_convert_fusion
  212.2 5.8 copy.127
  217.9 3.3 slice_bitcast_fusion
  221.2 3.7 copy.129
  224.9 2.4 copy.130
  227.3 2.5 copy.131
  230.9 64.8 %while.28 = (s32[]{:T(128)}, bf16[12,768,64]{1,2,0:T(8,128)(2,1)}, f32[12,768]{1,0:T(8,128)}, bf16[12,768,64]{2,1,0:T(8,128)(2,1)}, bf16[12,768,64]{2,1,0:T(8,12...) while((s32[]{:T(128)}, bf16[12,768,64]{1,2,0:T(8,128)(2,1)}, ...), condition=%wide.region_8.9_spmd.clone, body=%wide.region_5.8_spmd.clone.sunk | while | flops 156302592 | bytes 7911521 | solution.py:150
  239.6 2.2 fusion.143
  245.1 2.1 fusion.143
  250.5 2.1 fusion.143
  255.9 2.1 fusion.143
  266.6 2.1 fusion.143
  277.4 2.1 fusion.143
  295.7 3.2 fusion.89
  304.5 3.7 reshape.250
  308.2 5.2 fusion.90
  313.5 5.4 all-gather.16.cloned.1.call-done
  318.9 11.2 all-gather.14.cloned.1.call-done
  330.1 27.0 %multiply_convert_fusion.1 = (bf16[1536,1536]{1,0:T(8,128)(2,1)}, f32[1536,1536]{1,0:T(8,128)}, f32[1536,1536]{1,0:T(8,128)}) fusion(bf16[1536,768]{0,1:T(8,128)(2,1)} %all-gather.14.cloned.1.call-done, bf16[1536,768]{1,0:T(8,128)(2,1)} %all-gather.16.cloned.1.call-done), kind=kOutput, calls=%fused_computation.57 | convolution fusion | flops 3777232896 | bytes 28311552 | tf_op jit(solution)/shard_map/dot_general | solution.py:19
  357.1 9.2 fusion.95
  366.4 138.8 %reduce-scatter.11.cloned.1.call-done = f32[96,768]{1,0:T(8,128)} async-done(((f32[1536,768]{1,0:T(8,128)}), f32[96,768]{1,0:T(8,128)}) %reduce-scatter.11.cloned.1.call-update) | async-done | bytes 294928 | tf_op jit(solution)/shard_map/reduce_scatter | solution.py:192
  505.2 2.5 multiply_reduce_fusion.9
  508.0 62.5 %all-gather.18.cloned.1.call-done = bf16[1536,768]{1,0:T(8,128)(2,1)} async-done(((bf16[96,768]{1,0:T(8,128)(2,1)}), bf16[1536,768]{1,0:T(8,128)(2,1)}) %all-gather.18.cloned.1.call-update) | async-done | bytes 2359312 | tf_op jit(solution)/shard_map/all_gather | solution.py:135
  570.5 8.5 convolution_convert_fusion.1
  579.0 14.0 %add_convert_fusion = bf16[1536,1536]{1,0:T(8,128)(2,1)S(1)} fusion(f32[1536,1536]{1,0:T(8,128)} %get-tuple-element.433, bf16[1536,768]{0,1:T(8,128)(2,1)} %all-gather.22.cloned.1.call-done, bf16[1536,768]{1,0:T(8,128)(2,1)} %all-gather.18.cloned.1.call-done, f32[1536,1536]{1,0:T(8,128)} %get-tuple-element.462), kind=kOutput, calls=%fused_computation.56 | convolution fusion | flops 3656908800 | bytes 28311552 | tf_op jit(solution)/shard_map/dot_general | solution.py:19
  593.1 2.2 copy-done.69
  595.2 5.7 fusion.92
  601.5 9.4 fusion.94
  611.6 2.8 broadcast_select_fusion.3
  615.9 2.4 copy.148
  618.3 3.3 multiply_reduce_fusion.1
  629.6 107.8 %while.29 = (s32[]{:T(128)}, bf16[12,768,64]{1,2,0:T(8,128)(2,1)S(1)}, bf16[12,768,64]{1,2,0:T(8,128)(2,1)}, bf16[12,768,64]{1,2,0:T(8,128)(2,1)}, bf16[12,768,6...) while((s32[]{:T(128)}, ...), condition=%wide.region_17.18_spmd.clone, body=%wide.region_15.17_spmd.clone.sunk | while | flops 383483136 | bytes 19690608 | solution.py:201
  669.9 2.1 fusion.154
  723.8 2.1 fusion.154
  737.4 2.8 fusion.93
  741.7 2.1 maximum_convert_fusion
  745.7 5.5 fusion.76
  751.2 7.9 reshape.252
  759.1 7.4 fusion.91
  766.6 3.2 copy.140
  769.8 2.4 multiply_reduce_fusion.3
  774.6 2.6 add_add_fusion.2
  777.2 2.2 copy.144
  779.4 9.9 scatter_custom_fusion
  789.3 5.9 reshape.255
  797.0 2.6 broadcast_select_fusion.1
  799.7 41.4 %all-reduce.5 = f32[3072]{0:T(1024)S(1)} all-reduce(f32[3072]{0:T(1024)S(1)} %pad_maximum_fusion), channel_id=10, replica_groups=mesh['dp'=16,'tensor'=2] {'dp','tensor'}, use_global_device_ids=true, to_apply=%region_45.46.clone | all-reduce | flops 3072 | bytes 24576
  842.4 2.2 multiply_reduce_fusion.10
  844.6 239.9 %all-reduce.10.cloned.1.call-done = (f32[1769472]{0:T(1024)}, f32[589824]{0:T(1024)}, f32[786432]{0:T(1024)}, f32[1204224]{0:T(1024)}) async-done(((f32[1769472]{0:T(1024)}, f32[589824]{0:T(1024)}, f32[786432]{0:T(1024)}, f32[1204224]{0:T(1024)}), (f32[1769472]{0:T(1024)}, f32[589824]{0:T(1024)}, f32[786432]{0:T(1024)}, f32[1204224]{0:T(1024)})) %all-reduce.10.cloned.1.call-update) | async-done | bytes 17399824
  1084.6 2.7 multiply_reduce_fusion.12
  1087.2 2.5 multiply_reduce_fusion.14
  1089.7 2.2 multiply_reduce_fusion.16
  1091.9 2.2 multiply_reduce_fusion.18
  1094.1 4.5 stack.83
  1098.7 4.6 stack.91
  1104.7 39.6 %all-reduce.6 = (f32[7]{0:T(128)S(1)}, f32[7]{0:T(128)S(1)}) all-reduce(f32[7]{0:T(128)S(1)} %stack.91, f32[7]{0:T(128)S(1)} %stack.83), channel_id=1, replica_groups=mesh['dp'=16,'tensor'=2] {'dp','tensor'}, use_global_device_ids=true, to_apply=%region_47.48 | all-reduce | flops 14 | bytes 112 | tf_op jit(solution)/shard_map/psum | solution.py:250
  (380 shorter events, 209.9 us)
Async XLA Ops:
  7.2 9.9 copy-start.18
  7.2 11.3 copy-start.60
  7.2 54.9 %copy-start.59 = (s32[128]{0:T(128)S(1)}, s32[128]{0:T(128)}, u32[]{:S(2)}) copy-start(s32[128]{0:T(128)} %param.33) | copy-start | bytes 1540
  7.2 54.9 %copy-start.64 = (s32[128]{0:T(128)S(1)}, s32[128]{0:T(128)}, u32[]{:S(2)}) copy-start(s32[128]{0:T(128)} %param.34) | copy-start | bytes 1540
  7.2 61.2 %all-gather.12.cloned.1.call-start = ((), (), s32[]{:S(2)}) async-start(), calls=%async_computation.5 | async-start | bytes 1216512 | tf_op jit(solution)/shard_map/all_gather | solution.py:128
  8.9 126.1 %all-gather.24.cloned.1.call-start = ((), (), s32[]{:S(2)}) async-start(), calls=%async_computation.15 | async-start | bytes 4967424 | tf_op jit(solution)/shard_map/all_gather | solution.py:130
  10.6 186.7 %all-gather.10.cloned.1.call-start = ((), (), s32[]{:S(2)}) async-start(), calls=%async_computation.4 | async-start | bytes 3649536 | tf_op jit(solution)/shard_map/all_gather | solution.py:127
  12.3 292.2 %all-gather.20.cloned.1.call-start = ((), (), s32[]{:S(2)}) async-start(), calls=%async_computation.10 | async-start | bytes 1622016 | tf_op jit(solution)/shard_map/all_gather | solution.py:129
  13.9 305.0 %all-gather.16.cloned.1.call-start = ((), (), s32[]{:S(2)}) async-start(), calls=%async_computation.7 | async-start | bytes 2506752 | tf_op jit(solution)/shard_map/all_gather | solution.py:134
  15.6 314.5 %all-gather.14.cloned.1.call-start = ((), (), s32[]{:S(2)}) async-start(), calls=%async_computation.6 | async-start | bytes 3538944 | tf_op jit(solution)/shard_map/all_gather | solution.py:157
  17.1 187.9 %copy-start.51 = (pred[768]{0:T(1024)(128)(4,1)}, pred[768]{0:T(1024)(128)(4,1)S(1)}, u32[]{:S(2)}) copy-start(pred[768]{0:T(1024)(128)(4,1)S(1)} %compare_and_fusion) | copy-start | bytes 2308
  62.2 142.8 %copy-start.43 = (f32[768]{0:T(1024)}, f32[768]{0:T(1024)S(1)}, u32[]{:S(2)}) copy-start(f32[768]{0:T(1024)S(1)} %get-tuple-element.446) | copy-start | bytes 9220
  62.2 142.8 %copy-start.57 = (f32[768]{0:T(1024)}, f32[768]{0:T(1024)S(1)}, u32[]{:S(2)}) copy-start(f32[768]{0:T(1024)S(1)} %get-tuple-element.447) | copy-start | bytes 9220
  196.3 8.7 copy-start.2
  196.7 8.3 copy-start.36
  197.3 7.7 copy-start.45
  197.3 7.7 copy-start.49
  301.3 55.8 %all-gather.22.cloned.1.call-start = ((), (), s32[]{:S(2)}) async-start(), calls=%async_computation.11 | async-start | bytes 3538944 | tf_op jit(solution)/shard_map/all_gather | solution.py:178
  303.2 5.0 copy-start.21
  313.4 191.8 %reduce-scatter.11.cloned.1.call-start = ((), (), s32[]{:S(2)}) async-start(), calls=%async_computation.14 | async-start | bytes 5013504 | tf_op jit(solution)/shard_map/reduce_scatter | solution.py:192
  366.3 138.9 %copy-start.22 = (f32[96,768]{1,0:T(8,128)S(1)}, f32[96,768]{1,0:T(8,128)}, u32[]{:S(2)}) copy-start(f32[96,768]{1,0:T(8,128)} %param.49) | copy-start | bytes 884740
  366.3 138.9 %copy-start.32 = (f32[96,768]{1,0:T(8,128)S(1)}, f32[96,768]{1,0:T(8,128)}, u32[]{:S(2)}) copy-start(f32[96,768]{1,0:T(8,128)} %param.51) | copy-start | bytes 884740
  366.3 138.9 %copy-start.33 = (f32[96,768]{1,0:T(8,128)S(1)}, f32[96,768]{1,0:T(8,128)}, u32[]{:S(2)}) copy-start(f32[96,768]{1,0:T(8,128)} %param.50) | copy-start | bytes 884740
  366.4 204.1 %all-gather.18.cloned.1.call-start = ((), (), s32[]{:S(2)}) async-start(), calls=%async_computation.8 | async-start | bytes 2506752 | tf_op jit(solution)/shard_map/all_gather | solution.py:135
  507.8 103.2 %reduce-scatter.5.cloned.1.call-start = ((), (), s32[]{:S(2)}) async-start(), calls=%async_computation.9 | async-start | bytes 3538944 | tf_op jit(solution)/shard_map/reduce_scatter | solution.py:160
  579.0 39.3 %reduce-scatter.7.cloned.1.call-start = ((), (), s32[]{:S(2)}) async-start(), calls=%async_computation.12 | async-start | bytes 7077888 | tf_op jit(solution)/shard_map/reduce_scatter | solution.py:184
  579.0 16.2 %copy-start.67 = (bf16[1536,768]{1,0:T(8,128)(2,1)S(1)}, bf16[1536,768]{1,0:T(8,128)(2,1)}, u32[]{:S(2)}) copy-start(bf16[1536,768]{1,0:T(8,128)(2,1)} %all-gather.16.cloned.1.call-done) | copy-start | bytes 7077892
  601.0 241.4 %reduce-scatter.9.cloned.1.call-start = ((), (), s32[]{:S(2)}) async-start(), calls=%async_computation.13 | async-start | bytes 5013504 | tf_op jit(solution)/shard_map/reduce_scatter | solution.py:191
  610.9 473.7 %all-reduce.10.cloned.1.call-start = ((), (), s32[]{:S(2)}) async-start(), calls=%async_computation.16 | async-start | bytes 34799616
  611.6 2.8 copy-start.68
  618.3 3.3 copy-start.48
  618.3 3.3 copy-start.7
  741.7 3.9 copy-start.1
  741.7 3.9 copy-start.3
  741.7 3.9 copy-start.37
  741.7 3.9 copy-start.44
  741.7 3.9 copy-start.50
  741.7 3.9 copy-start.52
  741.7 3.9 copy-start.58
  766.6 3.2 copy-start.53
  769.7 2.5 copy-start.4
  779.4 9.9 copy-start.13
  797.0 2.7 copy-start.54
  797.0 2.7 copy-start.55
  797.0 44.2 %copy-start.61 = (f32[96]{0:T(128)S(1)}, f32[96]{0:T(128)}, u32[]{:S(2)}) copy-start(f32[96]{0:T(128)} %param.55) | copy-start | bytes 1156
  797.0 44.2 %copy-start.65 = (f32[96]{0:T(128)S(1)}, f32[96]{0:T(128)}, u32[]{:S(2)}) copy-start(f32[96]{0:T(128)} %param.57) | copy-start | bytes 1156
  797.0 44.1 %copy-start.66 = (f32[96]{0:T(128)S(1)}, f32[96]{0:T(128)}, u32[]{:S(2)}) copy-start(f32[96]{0:T(128)} %param.56) | copy-start | bytes 1156
  797.0 45.4 %copy-start.12 = (f32[96,768]{1,0:T(8,128)S(1)}, f32[96,768]{1,0:T(8,128)}, u32[]{:S(2)}) copy-start(f32[96,768]{1,0:T(8,128)} %param.46) | copy-start | bytes 884740
  797.0 287.6 %copy-start.14 = (f32[55296]{0:T(1024)S(1)}, f32[55296]{0:T(1024)}, u32[]{:S(2)}) copy-start(f32[55296]{0:T(1024)} %param.37) | copy-start | bytes 663556
  799.6 287.6 %copy-start.16 = (f32[37632]{0:T(1024)S(1)}, f32[37632]{0:T(1024)}, u32[]{:S(2)}) copy-start(f32[37632]{0:T(1024)} %param.52) | copy-start | bytes 451588
  799.6 287.6 %copy-start.34 = (f32[37632]{0:T(1024)S(1)}, f32[37632]{0:T(1024)}, u32[]{:S(2)}) copy-start(f32[37632]{0:T(1024)} %param.54) | copy-start | bytes 451588
  799.6 287.6 %copy-start.35 = (f32[37632]{0:T(1024)S(1)}, f32[37632]{0:T(1024)}, u32[]{:S(2)}) copy-start(f32[37632]{0:T(1024)} %param.53) | copy-start | bytes 451588
  799.6 290.1 %copy-start.30 = (f32[24576]{0:T(1024)S(1)}, f32[24576]{0:T(1024)}, u32[]{:S(2)}) copy-start(f32[24576]{0:T(1024)} %param.43) | copy-start | bytes 294916
  799.6 290.1 %copy-start.38 = (f32[24576]{0:T(1024)S(1)}, f32[24576]{0:T(1024)}, u32[]{:S(2)}) copy-start(f32[24576]{0:T(1024)} %param.45) | copy-start | bytes 294916
  799.6 290.1 %copy-start.39 = (f32[24576]{0:T(1024)S(1)}, f32[24576]{0:T(1024)}, u32[]{:S(2)}) copy-start(f32[24576]{0:T(1024)} %param.44) | copy-start | bytes 294916
  799.6 292.3 %copy-start.31 = (f32[18432]{0:T(1024)S(1)}, f32[18432]{0:T(1024)}, u32[]{:S(2)}) copy-start(f32[18432]{0:T(1024)} %param.40) | copy-start | bytes 221188
  799.7 292.3 %copy-start.40 = (f32[18432]{0:T(1024)S(1)}, f32[18432]{0:T(1024)}, u32[]{:S(2)}) copy-start(f32[18432]{0:T(1024)} %param.42) | copy-start | bytes 221188
  799.7 292.3 %copy-start.41 = (f32[18432]{0:T(1024)S(1)}, f32[18432]{0:T(1024)}, u32[]{:S(2)}) copy-start(f32[18432]{0:T(1024)} %param.41) | copy-start | bytes 221188
  842.4 260.9 %copy-start.10 = (bf16[768,768]{0,1:T(8,128)(2,1)S(1)}, bf16[768,768]{0,1:T(8,128)(2,1)}, u32[]{:S(2)}) copy-start(bf16[768,768]{0,1:T(8,128)(2,1)} %get-tuple-element.430) | copy-start | bytes 3538948
  844.6 312.8 %copy-start.28 = (f32[96,768]{1,0:T(8,128)}, f32[96,768]{1,0:T(8,128)S(1)}, u32[]{:S(2)}) copy-start(f32[96,768]{1,0:T(8,128)S(1)} %get-tuple-element.420) | copy-start | bytes 884740
  844.6 312.8 %copy-start.29 = (f32[96,768]{1,0:T(8,128)}, f32[96,768]{1,0:T(8,128)S(1)}, u32[]{:S(2)}) copy-start(f32[96,768]{1,0:T(8,128)S(1)} %get-tuple-element.421) | copy-start | bytes 884740
  1094.1 63.3 %copy-start.23 = (f32[96,768]{1,0:T(8,128)S(1)}, f32[96,768]{1,0:T(8,128)}, u32[]{:S(2)}) copy-start(f32[96,768]{1,0:T(8,128)} %param.49) | copy-start | bytes 884740
  1094.1 63.3 %copy-start.24 = (f32[96,768]{1,0:T(8,128)S(1)}, f32[96,768]{1,0:T(8,128)}, u32[]{:S(2)}) copy-start(f32[96,768]{1,0:T(8,128)} %get-tuple-element.418) | copy-start | bytes 884740
  1094.1 63.3 %copy-start.25 = (f32[96,768]{1,0:T(8,128)S(1)}, f32[96,768]{1,0:T(8,128)}, u32[]{:S(2)}) copy-start(f32[96,768]{1,0:T(8,128)} %get-tuple-element.419) | copy-start | bytes 884740
  (19 other events, 29.3 us)
Sparse Core Ops, SparseCore 0:
  11.6 56.8 all-gather.11
  71.8 63.1 all-gather.23
  138.4 58.8 all-gather.9
  200.6 53.7 all-gather.19
  257.7 61.1 all-gather.15
  320.3 9.7 all-gather.13
  331.6 12.1 all-gather.21
  366.5 138.6 reduce-scatter.10
  508.9 61.4 all-gather.17
  579.1 8.7 reduce-scatter.4
  601.1 11.3 reduce-scatter.6
  618.4 138.7 reduce-scatter.8
  795.4 289.1 all-reduce.9
where the time goes:
time: 1180 us; the launch traced here: 1170 us
  waiting for transfers between devices  526 us (45%)
  matrix products  248 us (21%)
  other arithmetic  125 us (11%)
  blocking collectives  123 us (10%)
  local copies, waits for them, and re-layouts  122 us (10%)
  between operations  19.4 us (2%)
    unnamed x14, waiting for transfers between devices  240 us
    dot_general x70, matrix products, contract(): lax.dot_general(left, right, (((left_dim,), (right_dim,)), ((), ())), pre...  180 us
    reduce_scatter x1, waiting for transfers between devices, local(): lax.psum_scatter(grad_reduce, 'dp', scatter_dimension=0, tiled=True)  139 us
    unnamed x2, blocking collectives  83.7 us
    all_gather x1, waiting for transfers between devices, local(): lax.all_gather(position_table.astype(jnp.bfloat16), ('dp', 'tensor'), axi...  63.2 us
    all_gather x1, waiting for transfers between devices, local(): lax.all_gather(reduce_weight.astype(jnp.bfloat16), 'dp', axis=0, tiled=True)  62.5 us
    all_gather x1, other arithmetic, local(): lax.all_gather(position_table.astype(jnp.bfloat16), ('dp', 'tensor'), axi...  51.2 us
    psum x1, blocking collectives, local(): lax.psum((jnp.stack([jnp.sum(master * master) for master in masters]), up...  39.6 us
  transfers between devices with their start and end apart: 13, of which 7 were waited for; matrix products, arithmetic and copies ran while one was open for 37% of the time, Pallas kernels for 0%

commit v1 on v0

--- a/solution.py
+++ b/solution.py
@@ -13,6 +13,16 @@
 ADAM_EPS = 1e-06
 DECAY = 0.05
 TINY = 1e-06
+
+
+def ring_gather(x, axis, dim):
+    ways, here, step = (lax.axis_size(axis), lax.axis_index(axis), x.shape[dim])
+    lengths = [n * ways if d == dim else n for d, n in enumerate(x.shape)]
+    full = lax.dynamic_update_slice_in_dim(jnp.zeros(lengths, x.dtype), x, here * step, axis=dim)
+    for far in range(1, ways):
+        x = lax.ppermute(x, axis, [(d, (d + 1) % ways) for d in range(ways)])
+        full = lax.dynamic_update_slice_in_dim(full, x, (here - far) % ways * step, axis=dim)
+    return full
 
 
 def contract(left, right, left_dim, right_dim):
@@ -132,7 +142,7 @@
     )
     expand_low, reduce_low = (
         lax.all_gather(expand_weight.astype(jnp.bfloat16), "dp", axis=0, tiled=True),
-        lax.all_gather(reduce_weight.astype(jnp.bfloat16), "dp", axis=0, tiled=True),
+        ring_gather(reduce_weight.astype(jnp.bfloat16), "dp", 0),
     )
     entry_low = gathered[0].reshape(model_width, 3 * model_width)
     exit_low = gathered[1].reshape(model_width, model_width)

time: 1180 us -> 1130 us (0.958)
  waiting for transfers between devices: 526 us -> 465 us
  local copies, waits for them, and re-layouts: 122 us -> 144 us
    ppermute x0 -> x15, waiting for transfers between devices: none -> 99.6 us  [ring_gather(): x = lax.ppermute(x, axis, [(d, (d + 1) % ways) for d in range(ways)])]
    reduce_scatter x1, waiting for transfers between devices: 139 us -> 46.9 us  [local(): lax.psum_scatter(grad_reduce, 'dp', scatter_dimension=0, tiled=True)]
    all_gather x1 -> x0, waiting for transfers between devices: 62.5 us -> none  [local(): lax.all_gather(reduce_weight.astype(jnp.bfloat16), 'dp', axis=0, tiled=True)]
    unnamed x14 -> x13, waiting for transfers between devices: 240 us -> 293 us
    all_gather x1, waiting for transfers between devices: 63.2 us -> 25.6 us  [local(): lax.all_gather(position_table.astype(jnp.bfloat16), ('dp', 'tensor'), axi...]
    dynamic_update_slice x0 -> x15, local copies, waits for them, and re-layouts: none -> 17.3 us  [ring_gather(): lax.dynamic_update_slice_in_dim(full, x, (here - far) % ways * step, axis...]
    unnamed x151 -> x159, local copies, waits for them, and re-layouts: 29.1 us -> 32.4 us
  transfers between devices with their start and end apart: 13 -> 27, of which waited for: 7 -> 16; matrix products, arithmetic and copies ran while one was open for 37% -> 42% of each run, Pallas kernels for 0% -> 0%
where the time goes in v1:
time: 1130 us; the launch traced here: 1120 us
  waiting for transfers between devices  465 us (41%)
  matrix products  246 us (22%)
  local copies, waits for them, and re-layouts  144 us (13%)
  other arithmetic  122 us (11%)
  blocking collectives  117 us (10%)
  between operations  19.8 us (2%)
    unnamed x13, waiting for transfers between devices  293 us
    dot_general x70, matrix products, contract(): lax.dot_general(left, right, (((left_dim,), (right_dim,)), ((), ())), pre...  181 us
    ppermute x15, waiting for transfers between devices, ring_gather(): x = lax.ppermute(x, axis, [(d, (d + 1) % ways) for d in range(ways)])  99.6 us
    unnamed x2, blocking collectives  77.8 us
    all_gather x1, other arithmetic, local(): lax.all_gather(position_table.astype(jnp.bfloat16), ('dp', 'tensor'), axi...  51.2 us
    reduce_scatter x1, waiting for transfers between devices, local(): lax.psum_scatter(grad_reduce, 'dp', scatter_dimension=0, tiled=True)  46.9 us
    psum x1, blocking collectives, local(): lax.psum((jnp.stack([jnp.sum(master * master) for master in masters]), up...  39.6 us
    unnamed x159, local copies, waits for them, and re-layouts  32.4 us
  transfers between devices with their start and end apart: 27, of which 16 were waited for; matrix products, arithmetic and copies ran while one was open for 42% of the time, Pallas kernels for 0%

profile of v1, /device:TPU:0, one launch (start us, length us, event | category | flops | bytes accessed | tf_op | source)
XLA Modules:
  0.0 1122.5 jit_solution(6927053213004350754)
XLA Ops:
  15.6 2.9 collective-permute-start
  21.3 40.6 %all-reduce = bf16[3072]{0:T(1024)(128)(2,1)S(1)} all-reduce(bf16[3072]{0:T(1024)(128)(2,1)S(1)} %dynamic-update-slice), channel_id=1, replica_groups=mesh['dp'=16,'tensor'=2] {'dp','tensor'}, use_global_device_ids=true, to_apply=%add | all-reduce | flops 3072 | bytes 12288
  61.9 2.3 collective-permute-start.1
  64.8 6.6 collective-permute-done.1
  71.4 8.7 collective-permute-done.2
  80.3 9.3 collective-permute-done.3
  90.2 8.0 collective-permute-done.4
  99.8 8.4 collective-permute-done.5
  108.6 3.3 reshape.249
  111.9 25.6 %all-gather.21.cloned.1.call-done = bf16[32,1,37632]{2,1,0:T(2,128)(2,1)} async-done(((bf16[1,1,37632]{2,1,0:T(2,128)(2,1)}), bf16[32,1,37632]{2,1,0:T(2,128)(2,1)}) %all-gather.21.cloned.1.call-update) | async-done | bytes 2408464 | tf_op jit(solution)/shard_map/all_gather | solution.py:140
  137.5 51.2 %reduce.1 = bf16[32,37632]{1,0:T(8,128)(2,1)} reduce(bf16[32,1,37632]{2,1,0:T(2,128)(2,1)} %all-gather.21.cloned.1.call-done, bf16[]{:T(256)} %constant.343), dimensions={1}, to_apply=%all-gather.reduce_sub_computation | reduce | bytes 4816898 | tf_op jit(solution)/shard_map/all_gather | solution.py:140
  188.7 5.0 reshape.244
  193.7 3.4 gather_fusion
  199.9 7.6 reshape.245
  207.6 6.7 convolution_convert_fusion
  214.3 6.3 copy.127
  220.6 3.3 slice_bitcast_fusion
  223.8 3.7 copy.129
  227.5 2.4 copy.130
  229.9 2.4 copy.131
  233.5 64.8 %while.28 = (s32[]{:T(128)}, bf16[12,768,64]{1,2,0:T(8,128)(2,1)}, f32[12,768]{1,0:T(8,128)}, bf16[12,768,64]{2,1,0:T(8,128)(2,1)}, bf16[12,768,64]{2,1,0:T(8,12...) while((s32[]{:T(128)}, bf16[12,768,64]{1,2,0:T(8,128)(2,1)}, ...), condition=%wide.region_8.9_spmd.clone, body=%wide.region_5.8_spmd.clone.sunk | while | flops 156302592 | bytes 7911521 | solution.py:160
  242.1 2.2 fusion.143
  298.3 3.2 fusion.89
  308.1 9.5 collective-permute-done.7
  320.7 9.2 collective-permute-done.8
  333.1 5.6 collective-permute-done.9
  341.9 5.6 collective-permute-done.10
  350.6 5.6 collective-permute-done.11
  357.5 7.4 collective-permute-done.12
  366.3 8.3 collective-permute-done.13
  375.9 7.4 collective-permute-done.14
  384.0 3.7 reshape.250
  387.7 5.2 fusion.90
  393.0 27.8 %multiply_convert_fusion.1 = (bf16[1536,1536]{1,0:T(8,128)(2,1)S(1)}, f32[1536,1536]{1,0:T(8,128)}, f32[1536,1536]{1,0:T(8,128)}) fusion(bf16[1536,768]{0,1:T(8,128)(2,1)} %all-gather.13.cloned.1.call-done, bf16[1536,768]{1,0:T(8,128)(2,1)} %all-gather.15.cloned.1.call-done), kind=kOutput, calls=%fused_computation.57 | convolution fusion | flops 3777232896 | bytes 28311552 | tf_op jit(solution)/shard_map/dot_general | solution.py:29
  420.8 2.2 copy-done.72
  423.0 5.4 convolution_convert_fusion.1
  428.5 14.6 %add_convert_fusion = bf16[1536,1536]{1,0:T(8,128)(2,1)S(1)} fusion(f32[1536,1536]{1,0:T(8,128)} %get-tuple-element.435, bf16[1536,768]{0,1:T(8,128)(2,1)} %all-gather.19.cloned.1.call-done, bf16[1536,768]{1,0:T(8,128)(2,1)} %constant_dynamic-update-slice_fusion, f32[1536,1536]{1,0:T(8,128)} %get-tuple-element.463), kind=kOutput, calls=%fused_computation.56 | convolution fusion | flops 3656908800 | bytes 28311552 | tf_op jit(solution)/shard_map/dot_general | solution.py:29
  445.3 5.7 fusion.92
  451.1 10.0 fusion.94
  461.5 9.1 fusion.95
  471.3 2.8 broadcast_select_fusion.3
  475.5 2.4 copy.148
  478.0 3.3 multiply_reduce_fusion.1
  489.4 107.5 %while.29 = (s32[]{:T(128)}, bf16[12,768,64]{1,2,0:T(8,128)(2,1)S(1)}, bf16[12,768,64]{1,2,0:T(8,128)(2,1)}, bf16[12,768,64]{1,2,0:T(8,128)(2,1)}, bf16[12,768,6...) while((s32[]{:T(128)}, ...), condition=%wide.region_17.18_spmd.clone, body=%wide.region_15.17_spmd.clone.sunk | while | flops 383483136 | bytes 19690608 | solution.py:211
  596.9 2.8 fusion.93
  605.1 5.5 fusion.76
  610.6 7.9 reshape.252
  618.5 7.4 fusion.91
  626.0 3.1 copy.140
  629.1 2.5 multiply_reduce_fusion.3
  634.0 2.6 add_add_fusion.2
  636.6 2.2 copy.144
  638.8 9.8 scatter_custom_fusion
  648.7 6.0 reshape.255
  656.5 2.6 broadcast_select_fusion.1
  659.0 37.1 %all-reduce.5 = f32[3072]{0:T(1024)S(1)} all-reduce(f32[3072]{0:T(1024)S(1)} %pad_maximum_fusion), channel_id=10, replica_groups=mesh['dp'=16,'tensor'=2] {'dp','tensor'}, use_global_device_ids=true, to_apply=%region_45.46.clone | all-reduce | flops 3072 | bytes 24576
  699.4 46.9 %reduce-scatter.11.cloned.1.call-done = f32[96,768]{1,0:T(8,128)} async-done(((f32[1536,768]{1,0:T(8,128)}), f32[96,768]{1,0:T(8,128)}) %reduce-scatter.11.cloned.1.call-update) | async-done | bytes 294928 | tf_op jit(solution)/shard_map/reduce_scatter | solution.py:202
  748.3 292.7 %all-reduce.10.cloned.1.call-done = (f32[1769472]{0:T(1024)}, f32[589824]{0:T(1024)}, f32[786432]{0:T(1024)}, f32[1204224]{0:T(1024)}) async-done(((f32[1769472]{0:T(1024)}, f32[589824]{0:T(1024)}, f32[786432]{0:T(1024)}, f32[1204224]{0:T(1024)}), (f32[1769472]{0:T(1024)}, f32[589824]{0:T(1024)}, f32[786432]{0:T(1024)}, f32[1204224]{0:T(1024)})) %all-reduce.10.cloned.1.call-update) | async-done | bytes 17399824
  1041.1 2.7 multiply_reduce_fusion.12
  1043.8 2.6 multiply_reduce_fusion.14
  1046.4 2.3 multiply_reduce_fusion.16
  1050.9 4.6 stack.83
  1055.6 4.6 stack.91
  1061.6 39.6 %all-reduce.6 = (f32[7]{0:T(128)S(1)}, f32[7]{0:T(128)S(1)}) all-reduce(f32[7]{0:T(128)S(1)} %stack.91, f32[7]{0:T(128)S(1)} %stack.83), channel_id=1, replica_groups=mesh['dp'=16,'tensor'=2] {'dp','tensor'}, use_global_device_ids=true, to_apply=%region_47.48 | all-reduce | flops 14 | bytes 112 | tf_op jit(solution)/shard_map/psum | solution.py:260
  (432 shorter events, 252.7 us)
Async XLA Ops:
  7.2 11.4 %copy-start.12 = (f32[96,768]{1,0:T(8,128)S(1)}, f32[96,768]{1,0:T(8,128)}, u32[]{:S(2)}) copy-start(f32[96,768]{1,0:T(8,128)} %param.46) | copy-start | bytes 884740
  7.2 101.3 %all-gather.11.cloned.1.call-start = ((), (), s32[]{:S(2)}) async-start(), calls=%async_computation.5 | async-start | bytes 1216512 | tf_op jit(solution)/shard_map/all_gather | solution.py:138
  8.9 10.5 copy-start.62
  8.9 10.5 copy-start.67
  8.9 128.6 %all-gather.21.cloned.1.call-start = ((), (), s32[]{:S(2)}) async-start(), calls=%async_computation.14 | async-start | bytes 4967424 | tf_op jit(solution)/shard_map/all_gather | solution.py:140
  10.6 9.8 copy-start.63
  10.6 60.8 %copy-start.59 = (s32[768]{0:T(1024)S(1)}, s32[768]{0:T(1024)}, u32[]{:S(2)}) copy-start(s32[768]{0:T(1024)} %param.32) | copy-start | bytes 9220
  10.6 87.7 %copy-start.23 = (bf16[768,768]{1,0:T(8,128)(2,1)S(1)}, bf16[768,768]{1,0:T(8,128)(2,1)}, u32[]{:S(2)}) copy-start(bf16[768,768]{1,0:T(8,128)(2,1)} %param.31) | copy-start | bytes 3538948
  10.6 189.3 %all-gather.9.cloned.1.call-start = ((), (), s32[]{:S(2)}) async-start(), calls=%async_computation.4 | async-start | bytes 3649536 | tf_op jit(solution)/shard_map/all_gather | solution.py:137
  12.4 371.6 %all-gather.17.cloned.1.call-start = ((), (), s32[]{:S(2)}) async-start(), calls=%async_computation.9 | async-start | bytes 1622016 | tf_op jit(solution)/shard_map/all_gather | solution.py:139
  14.0 379.0 %all-gather.15.cloned.1.call-start = ((), (), s32[]{:S(2)}) async-start(), calls=%async_computation.7 | async-start | bytes 2506752 | tf_op jit(solution)/shard_map/all_gather | solution.py:144
  15.6 46.3 %collective-permute-start = (bf16[96,768]{1,0:T(8,128)(2,1)S(1)}, bf16[96,768]{1,0:T(8,128)(2,1)S(1)}, u32[]{:S(2)}, u32[]{:S(2)}) collective-permute-start(bf16[96,768]{1,0:T(8,128)(2,1)S(1)} %get-tuple-element.433), channel_id=1, source_target_pairs={{0,2},{2,4},{4,6},{6,8},{8,10},{10,12},{12,14},{14,16},{16,18},{18... | collective-permute-start | bytes 442376 | tf_op jit(solution)/shard_map/ppermute | solution.py:23
  19.3 373.7 %all-gather.13.cloned.1.call-start = ((), (), s32[]{:S(2)}) async-start(), calls=%async_computation.6 | async-start | bytes 3538944 | tf_op jit(solution)/shard_map/all_gather | solution.py:167
  61.9 50.0 %copy-start.35 = (bf16[96,768]{1,0:T(8,128)(2,1)}, bf16[96,768]{1,0:T(8,128)(2,1)S(1)}, u32[]{:S(2)}) copy-start(bf16[96,768]{1,0:T(8,128)(2,1)S(1)} %collective-permute-done) | copy-start | bytes 442372
  61.9 9.4 collective-permute-start.1
  64.8 142.7 %copy-start.45 = (f32[768]{0:T(1024)}, f32[768]{0:T(1024)S(1)}, u32[]{:S(2)}) copy-start(f32[768]{0:T(1024)S(1)} %get-tuple-element.447) | copy-start | bytes 9220
  64.8 142.7 %copy-start.60 = (f32[768]{0:T(1024)}, f32[768]{0:T(1024)S(1)}, u32[]{:S(2)}) copy-start(f32[768]{0:T(1024)S(1)} %get-tuple-element.448) | copy-start | bytes 9220
  71.3 40.6 %copy-start.36 = (bf16[96,768]{1,0:T(8,128)(2,1)}, bf16[96,768]{1,0:T(8,128)(2,1)S(1)}, u32[]{:S(2)}) copy-start(bf16[96,768]{1,0:T(8,128)(2,1)S(1)} %collective-permute-done.1) | copy-start | bytes 442372
  71.3 8.7 collective-permute-start.2
  80.1 9.5 copy-start.37
  80.1 9.5 collective-permute-start.3
  89.5 22.4 %copy-start.38 = (bf16[96,768]{1,0:T(8,128)(2,1)}, bf16[96,768]{1,0:T(8,128)(2,1)S(1)}, u32[]{:S(2)}) copy-start(bf16[96,768]{1,0:T(8,128)(2,1)S(1)} %collective-permute-done.3) | copy-start | bytes 442372
  89.5 8.7 collective-permute-start.4
  98.3 13.6 %copy-start.39 = (bf16[96,768]{1,0:T(8,128)(2,1)}, bf16[96,768]{1,0:T(8,128)(2,1)S(1)}, u32[]{:S(2)}) copy-start(bf16[96,768]{1,0:T(8,128)(2,1)S(1)} %collective-permute-done.4) | copy-start | bytes 442372
  98.3 10.0 collective-permute-start.5
  98.3 109.2 %copy-start.53 = (pred[768]{0:T(1024)(128)(4,1)}, pred[768]{0:T(1024)(128)(4,1)S(1)}, u32[]{:S(2)}) copy-start(pred[768]{0:T(1024)(128)(4,1)S(1)} %compare_and_fusion) | copy-start | bytes 2308
  108.2 195.8 %collective-permute-start.6 = (bf16[96,768]{1,0:T(8,128)(2,1)}, bf16[96,768]{1,0:T(8,128)(2,1)}, u32[]{:S(2)}, u32[]{:S(2)}) collective-permute-start(bf16[96,768]{1,0:T(8,128)(2,1)} %collective-permute-done.5), channel_id=1, source_target_pairs={{0,2},{2,4},{4,6},{6,8},{8,10},{10,12},{12,14},{14,16},{16,18},{18... | collective-permute-start | bytes 442376 | tf_op jit(solution)/shard_map/ppermute | solution.py:23
  198.9 8.7 copy-start.2
  199.3 8.3 copy-start.40
  199.9 7.7 copy-start.47
  199.9 7.7 copy-start.51
  303.9 124.5 %all-gather.19.cloned.1.call-start = ((), (), s32[]{:S(2)}) async-start(), calls=%async_computation.10 | async-start | bytes 3538944 | tf_op jit(solution)/shard_map/all_gather | solution.py:188
  304.0 13.6 %collective-permute-start.7 = (bf16[96,768]{1,0:T(8,128)(2,1)}, bf16[96,768]{1,0:T(8,128)(2,1)}, u32[]{:S(2)}, u32[]{:S(2)}) collective-permute-start(bf16[96,768]{1,0:T(8,128)(2,1)} %collective-permute-done.6), channel_id=1, source_target_pairs={{0,2},{2,4},{4,6},{6,8},{8,10},{10,12},{12,14},{14,16},{16,18},{18... | collective-permute-start | bytes 442376 | tf_op jit(solution)/shard_map/ppermute | solution.py:23
  317.6 12.4 %collective-permute-start.8 = (bf16[96,768]{1,0:T(8,128)(2,1)}, bf16[96,768]{1,0:T(8,128)(2,1)S(1)}, u32[]{:S(2)}, u32[]{:S(2)}) collective-permute-start(bf16[96,768]{1,0:T(8,128)(2,1)} %collective-permute-done.7), channel_id=1, source_target_pairs={{0,2},{2,4},{4,6},{6,8},{8,10},{10,12},{12,14},{14,16},{16,18},{18... | collective-permute-start | bytes 442376 | tf_op jit(solution)/shard_map/ppermute | solution.py:23
  330.0 8.7 collective-permute-start.9
  338.7 8.7 collective-permute-start.10
  347.4 8.7 collective-permute-start.11
  356.2 8.7 collective-permute-start.12
  357.5 30.1 %copy-start.26 = (bf16[768,768]{0,1:T(8,128)(2,1)S(1)}, bf16[768,768]{0,1:T(8,128)(2,1)}, u32[]{:S(2)}) copy-start(bf16[768,768]{0,1:T(8,128)(2,1)} %copy.133) | copy-start | bytes 3538948
  364.9 9.7 collective-permute-start.13
  374.6 8.7 collective-permute-start.14
  392.9 77.8 %reduce-scatter.5.cloned.1.call-start = ((), (), s32[]{:S(2)}) async-start(), calls=%async_computation.8 | async-start | bytes 3538944 | tf_op jit(solution)/shard_map/reduce_scatter | solution.py:170
  393.0 30.0 %copy-start.17 = (bf16[1536,768]{1,0:T(8,128)(2,1)S(1)}, bf16[1536,768]{1,0:T(8,128)(2,1)}, u32[]{:S(2)}) copy-start(bf16[1536,768]{1,0:T(8,128)(2,1)} %constant_dynamic-update-slice_fusion) | copy-start | bytes 7077892
  428.4 49.6 %reduce-scatter.7.cloned.1.call-start = ((), (), s32[]{:S(2)}) async-start(), calls=%async_computation.11 | async-start | bytes 7077888 | tf_op jit(solution)/shard_map/reduce_scatter | solution.py:194
  428.5 16.8 %copy-start.70 = (bf16[1536,768]{1,0:T(8,128)(2,1)S(1)}, bf16[1536,768]{1,0:T(8,128)(2,1)}, u32[]{:S(2)}) copy-start(bf16[1536,768]{1,0:T(8,128)(2,1)} %all-gather.15.cloned.1.call-done) | copy-start | bytes 7077892
  451.0 246.4 %reduce-scatter.9.cloned.1.call-start = ((), (), s32[]{:S(2)}) async-start(), calls=%async_computation.12 | async-start | bytes 5013504 | tf_op jit(solution)/shard_map/reduce_scatter | solution.py:201
  461.0 285.3 %reduce-scatter.11.cloned.1.call-start = ((), (), s32[]{:S(2)}) async-start(), calls=%async_computation.13 | async-start | bytes 5013504 | tf_op jit(solution)/shard_map/reduce_scatter | solution.py:202
  470.6 570.5 %all-reduce.10.cloned.1.call-start = ((), (), s32[]{:S(2)}) async-start(), calls=%async_computation.15 | async-start | bytes 34799616
  638.8 9.9 copy-start.18
  656.4 39.8 %copy-start.64 = (f32[96]{0:T(128)S(1)}, f32[96]{0:T(128)}, u32[]{:S(2)}) copy-start(f32[96]{0:T(128)} %param.55) | copy-start | bytes 1156
  656.4 39.8 %copy-start.68 = (f32[96]{0:T(128)S(1)}, f32[96]{0:T(128)}, u32[]{:S(2)}) copy-start(f32[96]{0:T(128)} %param.57) | copy-start | bytes 1156
  656.4 39.7 %copy-start.69 = (f32[96]{0:T(128)S(1)}, f32[96]{0:T(128)}, u32[]{:S(2)}) copy-start(f32[96]{0:T(128)} %param.56) | copy-start | bytes 1156
  656.4 41.0 %copy-start.13 = (f32[96,768]{1,0:T(8,128)S(1)}, f32[96,768]{1,0:T(8,128)}, u32[]{:S(2)}) copy-start(f32[96,768]{1,0:T(8,128)} %param.46) | copy-start | bytes 884740
  656.4 89.9 %copy-start.15 = (f32[96,768]{1,0:T(8,128)S(1)}, f32[96,768]{1,0:T(8,128)}, u32[]{:S(2)}) copy-start(f32[96,768]{1,0:T(8,128)} %param.49) | copy-start | bytes 884740
  659.0 382.1 %copy-start.19 = (f32[55296]{0:T(1024)S(1)}, f32[55296]{0:T(1024)}, u32[]{:S(2)}) copy-start(f32[55296]{0:T(1024)} %param.37) | copy-start | bytes 663556
  697.4 346.4 %copy-start.21 = (f32[37632]{0:T(1024)S(1)}, f32[37632]{0:T(1024)}, u32[]{:S(2)}) copy-start(f32[37632]{0:T(1024)} %param.52) | copy-start | bytes 451588
  699.4 414.9 %copy-start.29 = (f32[96,768]{1,0:T(8,128)}, f32[96,768]{1,0:T(8,128)S(1)}, u32[]{:S(2)}) copy-start(f32[96,768]{1,0:T(8,128)S(1)} %get-tuple-element.420) | copy-start | bytes 884740
  699.4 414.9 %copy-start.30 = (f32[96,768]{1,0:T(8,128)}, f32[96,768]{1,0:T(8,128)S(1)}, u32[]{:S(2)}) copy-start(f32[96,768]{1,0:T(8,128)S(1)} %get-tuple-element.421) | copy-start | bytes 884740
  699.4 347.0 %copy-start.33 = (f32[24576]{0:T(1024)S(1)}, f32[24576]{0:T(1024)}, u32[]{:S(2)}) copy-start(f32[24576]{0:T(1024)} %param.43) | copy-start | bytes 294916
  699.4 349.3 %copy-start.34 = (f32[18432]{0:T(1024)S(1)}, f32[18432]{0:T(1024)}, u32[]{:S(2)}) copy-start(f32[18432]{0:T(1024)} %param.40) | copy-start | bytes 221188
  699.4 360.7 %copy-start.10 = (bf16[768,768]{0,1:T(8,128)(2,1)S(1)}, bf16[768,768]{0,1:T(8,128)(2,1)}, u32[]{:S(2)}) copy-start(bf16[768,768]{0,1:T(8,128)(2,1)} %get-tuple-element.430) | copy-start | bytes 3538948
  748.3 365.9 %copy-start.31 = (f32[96,768]{1,0:T(8,128)}, f32[96,768]{1,0:T(8,128)S(1)}, u32[]{:S(2)}) copy-start(f32[96,768]{1,0:T(8,128)S(1)} %get-tuple-element.418) | copy-start | bytes 884740
  748.3 365.9 %copy-start.32 = (f32[96,768]{1,0:T(8,128)}, f32[96,768]{1,0:T(8,128)S(1)}, u32[]{:S(2)}) copy-start(f32[96,768]{1,0:T(8,128)S(1)} %get-tuple-element.419) | copy-start | bytes 884740
  1041.1 7.7 copy-start.43
  (37 other events, 95.6 us)
Sparse Core Ops, SparseCore 0:
  11.5 56.9 all-gather.10
  71.9 65.6 all-gather.20
  141.0 58.8 all-gather.8
  203.2 53.7 all-gather.16
  260.2 64.4 all-gather.14
  326.2 13.5 all-gather.12
  393.1 6.8 all-gather.18
  428.5 5.7 reduce-scatter.4
  451.1 8.4 reduce-scatter.6
  464.7 138.8 reduce-scatter.8
  609.5 136.7 reduce-scatter.10
  752.6 288.4 all-reduce.9
